TPU v7x, 32 devices: a whole 2x2x4 slice. The times are simulated.
32 devices in a mesh: row: 4 (over x, core), col: 8 (over z, y).
Axes of the slice: x: 2, y: 2, z: 4, core: 2. Of those that a mesh axis runs over, the one named last changes fastest.
Arguments:
- panel: bfloat16 [3072, 98304], P('row', 'col'), may hold values from -0.01953125 to 0.01953125
- surface: bfloat16 [98304, 1024], P('col'), may hold values from -6 to 6
- flexibility: float32 [4, 768, 768], P('row'), may hold values from -0.21875 to 0.21875
- owner_map: int32 [24], replicated, may hold values from 0 to 23, each once
- adjacency: int32 [4, 2], P('row'), may hold values from 0 to 3, as said below
- live_rows: int32 [24], replicated, may hold values from 1 to 128, 2304 in all
Outputs:
- response: float32 [1024, 98304], P('row', 'col')
Inputs may be any that keep to these rules, and one draw needn't show every extreme that they name: `adjacency`: each substructure lists 2 different neighbours, never itself. `owner_map`: every slot receives exactly one mortar block. `live_rows`: the live rows add up to 2304 and some block is full.
All inputs are finite; a program needn't handle non-finite values.
Results may differ from a plain program's by a relative error of at most 0.0029.
Values may be sent and summed in bfloat16 or wider, within the bound.
A program may use at most 192 MiB of HBM per device.

v0:
```python
import math
import jax
import jax.numpy as jnp
from jax import lax
from jax.sharding import PartitionSpec as P

MBLK = 128
ITERS = 2
DAMPING = 0.6
COUPLING = 0.5


def live_pattern(live_rows):
    offsets = jnp.arange(MBLK, dtype=jnp.int32)
    return (offsets[None, :] < live_rows[:, None]).astype(jnp.float32)


def body(panel, surface, flexibility, owner_map, adjacency, live_rows):
    order_rows, column_count = panel.shape
    row_total = lax.axis_size("row")
    col_total = lax.axis_size("col")
    own_row = lax.axis_index("row")
    load_total = surface.shape[1]
    load_share = load_total // col_total
    block_count = order_rows // MBLK
    traction = lax.psum_scatter(
        lax.dot_general(
            surface, panel, (((0,), (1,)), ((), ())), preferred_element_type=jnp.float32
        ),
        "col",
        scatter_dimension=0,
        tiled=True,
    )
    pattern = live_pattern(live_rows)
    own_pattern = lax.dynamic_slice_in_dim(pattern, own_row * block_count, block_count, 0)
    blocks = traction.reshape(load_share, block_count, MBLK) * own_pattern[None]
    every_block = lax.all_gather(blocks, "row", axis=1, tiled=True)
    block_total = owner_map.shape[0]
    inverse = (
        jnp.zeros((block_total,), jnp.int32)
        .at[owner_map]
        .set(jnp.arange(block_total, dtype=jnp.int32))
    )
    own_sources = lax.dynamic_slice_in_dim(inverse, own_row * block_count, block_count, 0)
    load_blocks = jnp.take(every_block, own_sources, axis=1).reshape(load_share, order_rows)
    hits = adjacency[0][:, None] == jnp.arange(row_total, dtype=jnp.int32)[None, :]
    neighbour_weights = jnp.sum(hits.astype(jnp.float32), axis=0)
    flex_local = flexibility[0]
    traces = jnp.zeros_like(load_blocks)
    for sweep_index in range(ITERS):
        coupled = load_blocks
        if sweep_index > 0:
            neighbours = lax.all_gather(traces[None], "row", axis=0, tiled=True)
            coupled = load_blocks + COUPLING * jnp.einsum(
                "n,nlo->lo", neighbour_weights, neighbours, precision=lax.Precision.HIGHEST
            )
        applied = lax.dot_general(
            coupled,
            flex_local,
            (((1,), (1,)), ((), ())),
            precision=lax.Precision.HIGHEST,
            preferred_element_type=jnp.float32,
        )
        traces = (1.0 - DAMPING) * traces + DAMPING * applied
    rounded = traces.astype(jnp.bfloat16).reshape(load_share, block_count, MBLK)
    every_trace = lax.all_gather(rounded, "row", axis=1, tiled=True)
    own_slots = lax.dynamic_slice_in_dim(owner_map, own_row * block_count, block_count, 0)
    updated = (
        jnp.take(every_trace, own_slots, axis=1) * own_pattern[None].astype(jnp.bfloat16)
    ).reshape(load_share, order_rows)
    all_loads = lax.all_gather(updated, "col", axis=0, tiled=True)
    gain_factor = math.sqrt(column_count * col_total / (order_rows * row_total))
    return lax.psum_scatter(
        gain_factor * jnp.dot(all_loads, panel, preferred_element_type=jnp.float32),
        "row",
        scatter_dimension=0,
        tiled=True,
    )


def solution(mesh):
    in_specs = (P("row", "col"), P("col", None), P("row", None, None), P(), P("row", None), P())
    out_specs = P("row", "col")
    return jax.shard_map(body, mesh=mesh, in_specs=in_specs, out_specs=out_specs, check_vma=False)
```

profile of v0, /device:TPU:0, one launch (start us, length us, event | category | flops | bytes accessed | tf_op | source)
XLA Modules:
  0.0 604.5 jit_solution(13668140794669306131)
XLA Ops:
  6.5 26.5 %fusion.25 = f32[1024,768]{1,0:T(8,128)} fusion(bf16[12288,1024]{1,0:T(8,128)(2,1)} %param.7, bf16[768,12288]{1,0:T(8,128)(2,1)} %param.6), kind=kOutput, calls=%fused_computation.40 | convolution fusion | flops 19327352832 | bytes 47185920 | tf_op jit(solution)/shard_map/dot_general | solution.py:27
  33.1 0.6 copy-done.3
  33.8 76.6 %reduce-scatter.3.cloned.1.call-done = f32[128,768]{1,0:T(8,128)} async-done(((f32[1024,768]{1,0:T(8,128)}), f32[128,768]{1,0:T(8,128)}) %reduce-scatter.3.cloned.1.call-update) | async-done | bytes 393232 | tf_op jit(solution)/shard_map/reduce_scatter | solution.py:26
  110.4 1.1 copy.21
  111.7 0.9 copy.22
  112.8 0.6 scatter_custom_fusion
  113.5 18.0 %all-gather.5.cloned.1.call-done = f32[128,24,128]{2,0,1:T(8,128)} async-done(((f32[128,6,128]{2,0,1:T(8,128)}), f32[128,24,128]{2,0,1:T(8,128)}) %all-gather.5.cloned.1.call-update) | async-done | bytes 1572880 | tf_op jit(solution)/shard_map/all_gather | solution.py:37
  131.6 2.0 gather_fusion
  133.8 2.8 broadcast_multiply_fusion
  136.7 0.2 all-gather.7.cloned.1.call-start
  137.0 0.7 fusion.20
  138.2 18.3 %all-gather.9.cloned.1.call-done = f32[512,768]{1,0:T(8,128)} async-done(((f32[128,768]{1,0:T(8,128)}), f32[512,768]{1,0:T(8,128)}) %all-gather.9.cloned.1.call-update) | async-done | bytes 1572880 | tf_op jit(solution)/shard_map/all_gather | solution.py:53
  156.5 5.7 fusion.4
  162.2 1.2 copy.29
  163.4 3.2 fusion.12
  166.6 1.1 copy.25
  167.7 0.2 copy.26
  167.9 8.6 %all_gather.14 = bf16[128,24,128]{2,0,1:T(8,128)(2,1)S(1)} all-gather(bf16[128,6,128]{2,0,1:T(8,128)(2,1)S(1)} %copy.26), channel_id=1, replica_groups=mesh['row'=4,'col'=8] {'row'}, dimensions={1}, use_global_device_ids=true | all-gather | bytes 983040 | tf_op jit(solution)/shard_map/all_gather | solution.py:66
  176.5 0.6 gather_fusion.1
  177.3 1.0 fusion.17
  178.2 0.3 reduce-scatter.5.cloned.1.call-start
  178.5 44.3 %all-gather.7.cloned.1.call-done = bf16[1024,768]{0,1:T(8,128)(2,1)} async-done(((bf16[128,768]{0,1:T(8,128)(2,1)}), bf16[1024,768]{0,1:T(8,128)(2,1)}) %all-gather.7.cloned.1.call-update) | async-done | bytes 1572880 | tf_op jit(solution)/shard_map/all_gather | solution.py:71
  222.8 30.3 %convolution_multiply_fusion = f32[1024,12288]{1,0:T(8,128)} fusion(bf16[1024,768]{0,1:T(8,128)(2,1)} %all-gather.7.cloned.1.call-done, bf16[768,12288]{1,0:T(8,128)(2,1)} %param.6), kind=kOutput, calls=%fused_computation.3 | convolution fusion | flops 19339935744 | bytes 70778880 | tf_op jit(solution)/shard_map/dot_general | solution.py:74
  253.1 344.8 %reduce-scatter.5.cloned.1.call-done = f32[256,12288]{1,0:T(8,128)} async-done(((f32[1024,12288]{1,0:T(8,128)}), f32[256,12288]{1,0:T(8,128)}) %reduce-scatter.5.cloned.1.call-update) | async-done | bytes 12582928 | tf_op jit(solution)/shard_map/reduce_scatter | solution.py:73
  (33 shorter events, 1.6 us)
Async XLA Ops:
  6.5 127.3 %copy-start = (f32[1,768,768]{2,1,0:T(8,128)S(1)}, f32[1,768,768]{2,1,0:T(8,128)}, u32[]{:S(2)}) copy-start(f32[1,768,768]{2,1,0:T(8,128)} %param.8) | copy-start | bytes 7077892
  6.5 103.9 %reduce-scatter.3.cloned.1.call-start = ((), (), s32[]{:S(2)}) async-start(), calls=%async_computation.2 | async-start | bytes 3538944 | tf_op jit(solution)/shard_map/reduce_scatter | solution.py:26
  33.0 0.7 copy-start.3
  33.0 79.7 %copy-start.2 = (s32[24]{0:T(128)S(1)}, s32[24]{0:T(128)}, u32[]{:S(2)}) copy-start(s32[24]{0:T(128)} %param.9) | copy-start | bytes 292
  33.1 98.5 %all-gather.5.cloned.1.call-start = ((), (), s32[]{:S(2)}) async-start(), calls=%async_computation.3 | async-start | bytes 1966080 | tf_op jit(solution)/shard_map/all_gather | solution.py:37
  112.7 43.8 %all-gather.9.cloned.1.call-start = ((), (), s32[]{:S(2)}) async-start(), calls=%async_computation.6 | async-start | bytes 1966080 | tf_op jit(solution)/shard_map/all_gather | solution.py:53
  113.5 23.5 %copy-start.4 = (s32[1,2]{1,0:T(1,128)S(1)}, s32[1,2]{1,0:T(1,128)}, u32[]{:S(2)}) copy-start(s32[1,2]{1,0:T(1,128)} %param.10) | copy-start | bytes 28
  136.7 86.1 %all-gather.7.cloned.1.call-start = ((), (), s32[]{:S(2)}) async-start(), calls=%async_computation.4 | async-start | bytes 1769472 | tf_op jit(solution)/shard_map/all_gather | solution.py:71
  178.2 419.7 %reduce-scatter.5.cloned.1.call-start = ((), (), s32[]{:S(2)}) async-start(), calls=%async_computation.5 | async-start | bytes 62914560 | tf_op jit(solution)/shard_map/reduce_scatter | solution.py:73
  253.1 344.9 %copy-start.1 = (f32[1,768,768]{2,1,0:T(8,128)S(1)}, f32[1,768,768]{2,1,0:T(8,128)}, u32[]{:S(2)}) copy-start(f32[1,768,768]{2,1,0:T(8,128)} %param.8) | copy-start | bytes 7077892
Sparse Core Ops, SparseCore 0:
  33.2 77.1 reduce-scatter.2
  112.8 18.7 all-gather.4
  136.8 19.6 all-gather.8
  178.4 44.4 all-gather.6
  253.2 344.6 reduce-scatter.4
where the time goes:
time: 605 us; the launch traced here: 604 us
  waiting for transfers between devices  502 us (83%)
  matrix products  68.5 us (11%)
  between operations  13.3 us (2%)
  local copies, waits for them, and re-layouts  9.05 us (1%)
  blocking collectives  8.58 us (1%)
    reduce_scatter x1, waiting for transfers between devices, body(): lax.psum_scatter(gain_factor * jnp.dot(all_loads, panel, preferred_elemen...  345 us
    reduce_scatter x1, waiting for transfers between devices, body(): lax.psum_scatter(lax.dot_general(surface, panel, (((0,), (1,)), ((), ()))...  76.6 us
    all_gather x1, waiting for transfers between devices, body(): all_loads = lax.all_gather(updated, 'col', axis=0, tiled=True)  44.3 us
    dot_general x1, matrix products, body(): jnp.dot(all_loads, panel, preferred_element_type=jnp.float32)  30.3 us
    dot_general x1, matrix products, body(): lax.dot_general(surface, panel, (((0,), (1,)), ((), ())), preferred_eleme...  26.5 us
    all_gather x1, waiting for transfers between devices, body(): neighbours = lax.all_gather(traces[None], 'row', axis=0, tiled=True)  18.3 us
    all_gather x1, waiting for transfers between devices, body(): every_block = lax.all_gather(blocks, 'row', axis=1, tiled=True)  18 us
  transfers between devices with their start and end apart: 5, of which 5 were waited for; matrix products, arithmetic and copies ran while one was open for 0% of the time, Pallas kernels for 0%

commit v1 on v0

--- a/solution.py
+++ b/solution.py
@@ -68,7 +68,14 @@
     updated = (
         jnp.take(every_trace, own_slots, axis=1) * own_pattern[None].astype(jnp.bfloat16)
     ).reshape(load_share, order_rows)
-    all_loads = lax.all_gather(updated, "col", axis=0, tiled=True)
+    devices = lax.axis_size("col")
+    right = [(i, (i + 1) % devices) for i in range(devices)]
+    pieces = [updated]
+    for stride in range(1, devices):
+        pieces = [lax.ppermute(pieces[0], "col", right), *pieces]
+    out = jnp.concatenate(pieces, axis=0)
+    places = (lax.axis_index("col") + 1) * pieces[-1].shape[0]
+    all_loads = jnp.roll(out, places, axis=0)
     gain_factor = math.sqrt(column_count * col_total / (order_rows * row_total))
     return lax.psum_scatter(
         gain_factor * jnp.dot(all_loads, panel, preferred_element_type=jnp.float32),

time: 605 us -> 630 us (1.041)
  waiting for transfers between devices: 502 us -> 516 us
  local copies, waits for them, and re-layouts: 9.05 us -> 20.1 us
    ppermute x0 -> x7, waiting for transfers between devices: none -> 59.9 us  [body(): pieces = [lax.ppermute(pieces[0], 'col', right), *pieces]]
    all_gather x1 -> x0, waiting for transfers between devices: 44.3 us -> none  [body(): all_loads = lax.all_gather(updated, 'col', axis=0, tiled=True)]
    unnamed x10 -> x25, local copies, waits for them, and re-layouts: 0.59 us -> 10.9 us
  transfers between devices with their start and end apart: 5 -> 11, of which waited for: 5 -> 11; matrix products, arithmetic and copies ran while one was open for 0% -> 0% of each run, Pallas kernels for 0% -> 0%
where the time goes in v1:
time: 630 us
  waiting for transfers between devices  516 us (82%)
  matrix products  68.6 us (11%)
  local copies, waits for them, and re-layouts  20.1 us (3%)
  between operations  13.3 us (2%)
  blocking collectives  8.58 us (1%)
    reduce_scatter x1, waiting for transfers between devices, body(): lax.psum_scatter(gain_factor * jnp.dot(all_loads, panel, preferred_elemen...  343 us
    reduce_scatter x1, waiting for transfers between devices, body(): lax.psum_scatter(lax.dot_general(surface, panel, (((0,), (1,)), ((), ()))...  76.6 us
    ppermute x7, waiting for transfers between devices, body(): pieces = [lax.ppermute(pieces[0], 'col', right), *pieces]  59.9 us
    dot_general x1, matrix products, body(): jnp.dot(all_loads, panel, preferred_element_type=jnp.float32)  30.4 us
    dot_general x1, matrix products, body(): lax.dot_general(surface, panel, (((0,), (1,)), ((), ())), preferred_eleme...  26.5 us
    all_gather x1, waiting for transfers between devices, body(): neighbours = lax.all_gather(traces[None], 'row', axis=0, tiled=True)  18.3 us
    all_gather x1, waiting for transfers between devices, body(): every_block = lax.all_gather(blocks, 'row', axis=1, tiled=True)  18 us
  transfers between devices with their start and end apart: 11, of which 11 were waited for; matrix products, arithmetic and copies ran while one was open for 0% of the time, Pallas kernels for 0%

profile of v1, /device:TPU:0, one launch (start us, length us, event | category | flops | bytes accessed | tf_op | source)
XLA Modules:
  0.0 629.9 jit_solution(14632227334438595398)
XLA Ops:
  6.5 26.5 %fusion.27 = f32[1024,768]{1,0:T(8,128)} fusion(bf16[12288,1024]{1,0:T(8,128)(2,1)} %param.7, bf16[768,12288]{1,0:T(8,128)(2,1)} %param.6), kind=kOutput, calls=%fused_computation.58 | convolution fusion | flops 19327352832 | bytes 47185920 | tf_op jit(solution)/shard_map/dot_general | solution.py:27
  33.8 76.6 %reduce-scatter.3.cloned.1.call-done = f32[128,768]{1,0:T(8,128)} async-done(((f32[1024,768]{1,0:T(8,128)}), f32[128,768]{1,0:T(8,128)}) %reduce-scatter.3.cloned.1.call-update) | async-done | bytes 393232 | tf_op jit(solution)/shard_map/reduce_scatter | solution.py:26
  110.4 1.1 copy.21
  111.7 0.9 copy.22
  113.5 18.0 %all-gather.4.cloned.1.call-done = f32[128,24,128]{2,0,1:T(8,128)} async-done(((f32[128,6,128]{2,0,1:T(8,128)}), f32[128,24,128]{2,0,1:T(8,128)}) %all-gather.4.cloned.1.call-update) | async-done | bytes 1572880 | tf_op jit(solution)/shard_map/all_gather | solution.py:37
  131.6 2.0 gather_fusion
  133.8 2.8 broadcast_multiply_fusion
  138.2 18.3 %all-gather.6.cloned.1.call-done = f32[512,768]{1,0:T(8,128)} async-done(((f32[128,768]{1,0:T(8,128)}), f32[512,768]{1,0:T(8,128)}) %all-gather.6.cloned.1.call-update) | async-done | bytes 1572880 | tf_op jit(solution)/shard_map/all_gather | solution.py:53
  156.5 5.7 fusion.4
  162.2 1.2 copy.29
  163.4 3.2 fusion.13
  166.6 1.1 copy.25
  167.9 8.6 %all_gather.11 = bf16[128,24,128]{2,0,1:T(8,128)(2,1)S(1)} all-gather(bf16[128,6,128]{2,0,1:T(8,128)(2,1)S(1)} %copy.26), channel_id=1, replica_groups=mesh['row'=4,'col'=8] {'row'}, dimensions={1}, use_global_device_ids=true | all-gather | bytes 983040 | tf_op jit(solution)/shard_map/all_gather | solution.py:66
  177.5 1.5 collective-permute-start
  179.1 8.4 %collective-permute-done = bf16[128,768]{0,1:T(8,128)(2,1)S(1)} collective-permute-done((bf16[128,768]{0,1:T(8,128)(2,1)S(1)}, bf16[128,768]{0,1:T(8,128)(2,1)S(1)}, u32[]{:S(2)}, u32[]{:S(2)}) %collective-permute-start) | collective-permute-done | bytes 196640 | tf_op jit(solution)/shard_map/ppermute | solution.py:75
  187.4 9.0 %collective-permute-done.1 = bf16[128,768]{0,1:T(8,128)(2,1)S(1)} collective-permute-done((bf16[128,768]{0,1:T(8,128)(2,1)S(1)}, bf16[128,768]{0,1:T(8,128)(2,1)S(1)}, u32[]{:S(2)}, u32[]{:S(2)}) %collective-permute-start.1) | collective-permute-done | bytes 196640 | tf_op jit(solution)/shard_map/ppermute | solution.py:75
  196.4 8.4 %collective-permute-done.2 = bf16[128,768]{0,1:T(8,128)(2,1)S(1)} collective-permute-done((bf16[128,768]{0,1:T(8,128)(2,1)S(1)}, bf16[128,768]{0,1:T(8,128)(2,1)S(1)}, u32[]{:S(2)}, u32[]{:S(2)}) %collective-permute-start.2) | collective-permute-done | bytes 196640 | tf_op jit(solution)/shard_map/ppermute | solution.py:75
  204.8 8.4 %collective-permute-done.3 = bf16[128,768]{0,1:T(8,128)(2,1)S(1)} collective-permute-done((bf16[128,768]{0,1:T(8,128)(2,1)S(1)}, bf16[128,768]{0,1:T(8,128)(2,1)S(1)}, u32[]{:S(2)}, u32[]{:S(2)}) %collective-permute-start.3) | collective-permute-done | bytes 196640 | tf_op jit(solution)/shard_map/ppermute | solution.py:75
  213.2 8.4 %collective-permute-done.4 = bf16[128,768]{0,1:T(8,128)(2,1)S(1)} collective-permute-done((bf16[128,768]{0,1:T(8,128)(2,1)S(1)}, bf16[128,768]{0,1:T(8,128)(2,1)S(1)}, u32[]{:S(2)}, u32[]{:S(2)}) %collective-permute-start.4) | collective-permute-done | bytes 196640 | tf_op jit(solution)/shard_map/ppermute | solution.py:75
  221.5 9.0 %collective-permute-done.5 = bf16[128,768]{0,1:T(8,128)(2,1)S(1)} collective-permute-done((bf16[128,768]{0,1:T(8,128)(2,1)S(1)}, bf16[128,768]{0,1:T(8,128)(2,1)S(1)}, u32[]{:S(2)}, u32[]{:S(2)}) %collective-permute-start.5) | collective-permute-done | bytes 196640 | tf_op jit(solution)/shard_map/ppermute | solution.py:75
  230.6 8.4 %collective-permute-done.6 = bf16[128,768]{0,1:T(8,128)(2,1)S(1)} collective-permute-done((bf16[128,768]{0,1:T(8,128)(2,1)S(1)}, bf16[128,768]{0,1:T(8,128)(2,1)S(1)}, u32[]{:S(2)}, u32[]{:S(2)}) %collective-permute-start.6) | collective-permute-done | bytes 196640 | tf_op jit(solution)/shard_map/ppermute | solution.py:75
  238.9 0.7 constant_dynamic-update-slice_fusion.15
  250.0 30.4 %convolution_multiply_fusion = f32[1024,12288]{1,0:T(8,128)} fusion(bf16[768,12288]{1,0:T(8,128)(2,1)} %param.6, bf16[2048,768]{0,1:T(8,128)(2,1)} %constant_dynamic-update-slice_fusion, s32[]{:T(128)S(6)} %select_n.60), kind=kOutput, calls=%fused_computation.3 | convolution fusion | flops 19339935744 | bytes 70778880 | tf_op jit(solution)/shard_map/dot_general | solution.py:81
  280.4 343.0 %reduce-scatter.5.cloned.1.call-done = f32[256,12288]{1,0:T(8,128)} async-done(((f32[1024,12288]{1,0:T(8,128)}), f32[256,12288]{1,0:T(8,128)}) %reduce-scatter.5.cloned.1.call-update) | async-done | bytes 12582928 | tf_op jit(solution)/shard_map/reduce_scatter | solution.py:80
  (60 shorter events, 15.1 us)
Async XLA Ops:
  6.5 127.3 %copy-start = (f32[1,768,768]{2,1,0:T(8,128)S(1)}, f32[1,768,768]{2,1,0:T(8,128)}, u32[]{:S(2)}) copy-start(f32[1,768,768]{2,1,0:T(8,128)} %param.8) | copy-start | bytes 7077892
  6.5 103.9 %reduce-scatter.3.cloned.1.call-start = ((), (), s32[]{:S(2)}) async-start(), calls=%async_computation.2 | async-start | bytes 3538944 | tf_op jit(solution)/shard_map/reduce_scatter | solution.py:26
  33.0 0.7 copy-start.3
  33.0 79.7 %copy-start.2 = (s32[24]{0:T(128)S(1)}, s32[24]{0:T(128)}, u32[]{:S(2)}) copy-start(s32[24]{0:T(128)} %param.9) | copy-start | bytes 292
  33.1 98.5 %all-gather.4.cloned.1.call-start = ((), (), s32[]{:S(2)}) async-start(), calls=%async_computation.3 | async-start | bytes 1966080 | tf_op jit(solution)/shard_map/all_gather | solution.py:37
  112.7 43.8 %all-gather.6.cloned.1.call-start = ((), (), s32[]{:S(2)}) async-start(), calls=%async_computation.5 | async-start | bytes 1966080 | tf_op jit(solution)/shard_map/all_gather | solution.py:53
  113.5 23.5 %copy-start.4 = (s32[1,2]{1,0:T(1,128)S(1)}, s32[1,2]{1,0:T(1,128)}, u32[]{:S(2)}) copy-start(s32[1,2]{1,0:T(1,128)} %param.10) | copy-start | bytes 28
  136.7 486.6 %reduce-scatter.5.cloned.1.call-start = ((), (), s32[]{:S(2)}) async-start(), calls=%async_computation.4 | async-start | bytes 62914560 | tf_op jit(solution)/shard_map/reduce_scatter | solution.py:80
  177.5 9.9 %collective-permute-start = (bf16[128,768]{0,1:T(8,128)(2,1)S(1)}, bf16[128,768]{0,1:T(8,128)(2,1)S(1)}, u32[]{:S(2)}, u32[]{:S(2)}) collective-permute-start(bf16[128,768]{0,1:T(8,128)(2,1)S(1)} %fusion.18), channel_id=1, source_target_pairs={{0,1},{1,2},{2,3},{3,4},{4,5},{5,6},{6,7},{7,0},{8,9},{9,10},{10,1... | collective-permute-start | bytes 589832 | tf_op jit(solution)/shard_map/ppermute | solution.py:75
  187.4 9.0 %collective-permute-start.1 = (bf16[128,768]{0,1:T(8,128)(2,1)S(1)}, bf16[128,768]{0,1:T(8,128)(2,1)S(1)}, u32[]{:S(2)}, u32[]{:S(2)}) collective-permute-start(bf16[128,768]{0,1:T(8,128)(2,1)S(1)} %collective-permute-done), channel_id=1, source_target_pairs={{0,1},{1,2},{2,3},{3,4},{4,5},{5,6},{6,7},{7,0},{8,9},{9,10},{10,1... | collective-permute-start | bytes 589832 | tf_op jit(solution)/shard_map/ppermute | solution.py:75
  196.4 8.4 %collective-permute-start.2 = (bf16[128,768]{0,1:T(8,128)(2,1)S(1)}, bf16[128,768]{0,1:T(8,128)(2,1)S(1)}, u32[]{:S(2)}, u32[]{:S(2)}) collective-permute-start(bf16[128,768]{0,1:T(8,128)(2,1)S(1)} %collective-permute-done.1), channel_id=1, source_target_pairs={{0,1},{1,2},{2,3},{3,4},{4,5},{5,6},{6,7},{7,0},{8,9},{9,10},{10,1... | collective-permute-start | bytes 589832 | tf_op jit(solution)/shard_map/ppermute | solution.py:75
  204.8 8.4 %collective-permute-start.3 = (bf16[128,768]{0,1:T(8,128)(2,1)S(1)}, bf16[128,768]{0,1:T(8,128)(2,1)S(1)}, u32[]{:S(2)}, u32[]{:S(2)}) collective-permute-start(bf16[128,768]{0,1:T(8,128)(2,1)S(1)} %collective-permute-done.2), channel_id=1, source_target_pairs={{0,1},{1,2},{2,3},{3,4},{4,5},{5,6},{6,7},{7,0},{8,9},{9,10},{10,1... | collective-permute-start | bytes 589832 | tf_op jit(solution)/shard_map/ppermute | solution.py:75
  213.2 8.4 %collective-permute-start.4 = (bf16[128,768]{0,1:T(8,128)(2,1)S(1)}, bf16[128,768]{0,1:T(8,128)(2,1)S(1)}, u32[]{:S(2)}, u32[]{:S(2)}) collective-permute-start(bf16[128,768]{0,1:T(8,128)(2,1)S(1)} %collective-permute-done.3), channel_id=1, source_target_pairs={{0,1},{1,2},{2,3},{3,4},{4,5},{5,6},{6,7},{7,0},{8,9},{9,10},{10,1... | collective-permute-start | bytes 589832 | tf_op jit(solution)/shard_map/ppermute | solution.py:75
  221.5 9.0 %collective-permute-start.5 = (bf16[128,768]{0,1:T(8,128)(2,1)S(1)}, bf16[128,768]{0,1:T(8,128)(2,1)S(1)}, u32[]{:S(2)}, u32[]{:S(2)}) collective-permute-start(bf16[128,768]{0,1:T(8,128)(2,1)S(1)} %collective-permute-done.4), channel_id=1, source_target_pairs={{0,1},{1,2},{2,3},{3,4},{4,5},{5,6},{6,7},{7,0},{8,9},{9,10},{10,1... | collective-permute-start | bytes 589832 | tf_op jit(solution)/shard_map/ppermute | solution.py:75
  230.6 8.4 %collective-permute-start.6 = (bf16[128,768]{0,1:T(8,128)(2,1)S(1)}, bf16[128,768]{0,1:T(8,128)(2,1)S(1)}, u32[]{:S(2)}, u32[]{:S(2)}) collective-permute-start(bf16[128,768]{0,1:T(8,128)(2,1)S(1)} %collective-permute-done.5), channel_id=1, source_target_pairs={{0,1},{1,2},{2,3},{3,4},{4,5},{5,6},{6,7},{7,0},{8,9},{9,10},{10,1... | collective-permute-start | bytes 589832 | tf_op jit(solution)/shard_map/ppermute | solution.py:75
  280.4 343.0 %copy-start.1 = (f32[1,768,768]{2,1,0:T(8,128)S(1)}, f32[1,768,768]{2,1,0:T(8,128)}, u32[]{:S(2)}) copy-start(f32[1,768,768]{2,1,0:T(8,128)} %param.8) | copy-start | bytes 7077892
Sparse Core Ops, SparseCore 0:
  33.2 77.1 reduce-scatter.2
  112.8 18.7 all-gather.3
  136.8 19.6 all-gather.5
  280.5 342.8 reduce-scatter.4
